TPU v7x, 32 devices: a whole 2x2x4 slice. The times are simulated.
32 devices in a mesh: groups: 2 (over y), ctx: 4 (over z), tm: 2 (over x), tp: 2 (over core).
Axes of the slice: x: 2, y: 2, z: 4, core: 2. Of those that a mesh axis runs over, the one named last changes fastest.
Arguments:
- tokens: bfloat16 [256, 8, 1024], P(('groups', 'tm'), 'ctx'), parts along dimension 0, may hold values from -6 to 6
- norm_gain: float32 [1024], replicated, may hold values from 0.1 to 1.9
- block_mask: int32 [4, 4, 4], P(('groups', 'tm'), 'ctx'), parts along dimension 0, may hold values from 0 to 1, as said below
- w_query: bfloat16 [1024, 1024], P('tm', 'tp'), may hold values from -1.25 to 1.25
- w_key: bfloat16 [1024, 1024], P('tm', 'tp'), may hold values from -1.25 to 1.25
- w_value: bfloat16 [1024, 1024], P('tm', 'tp'), may hold values from -0.1875 to 0.1875
- w_out: bfloat16 [1024, 1024], P('tp', 'tm'), may hold values from -0.1875 to 0.1875
- w_up: bfloat16 [1024, 2048], P('tm', 'tp'), may hold values from -0.1875 to 0.1875
- w_down: bfloat16 [2048, 1024], P('tp', 'tm'), may hold values from -0.125 to 0.125
- conv_weight: float32 [5, 1024], P(None, 'tp'), may hold values from -2.5 to 2.5
Outputs:
- denoised: bfloat16 [256, 8, 1024], P(('groups', 'tm'), 'ctx', 'tp'), parts along dimension 0
There are 2 independent parts, one for each index of `groups`. A program takes and returns all parts, laid end to end along the dimension named above; an argument that names none is the same for every part. Nothing has to cross between parts.
Inputs may be any that keep to these rules, and one draw needn't show every extreme that they name: block_mask[w, i, i] is 1 for every window w and block i.
All inputs are finite; a program needn't handle non-finite values.
Results may differ from a plain program's by a relative error of at most 0.0076.
Values may be sent and summed in bfloat16 or wider, within the bound.
A program may use at most 64 MiB of HBM per device.

v0:
```python
import jax
import jax.numpy as jnp
from jax import lax
from jax.sharding import PartitionSpec as P

HEAD_DIM = 64
KERNEL = 5


def from_behind(value, axis, steps):
    count = lax.axis_size(axis)
    first, last = (max(0, -steps), min(count, count - steps))
    return lax.ppermute(value, axis, [(source, source + steps) for source in range(first, last)])


def rms_norm(tokens, norm_gain):
    values = tokens.astype(jnp.float32)
    square = jnp.mean(values * values, axis=-1, keepdims=True)
    return (values * lax.rsqrt(square + 1e-05) * norm_gain).astype(jnp.bfloat16)


def on_device(
    tokens, norm_gain, block_mask, w_query, w_key, w_value, w_out, w_up, w_down, conv_weight
):
    frames_here, dancers_here, width = tokens.shape
    rows_here = frames_here * dancers_here
    normed_grid = rms_norm(tokens, norm_gain)
    normed = normed_grid.reshape(rows_here, width)
    pieces = (
        lax.all_gather(w_query, "tm", axis=0, tiled=True),
        lax.all_gather(w_key, "tm", axis=0, tiled=True),
        lax.all_gather(w_value, "tm", axis=0, tiled=True),
        lax.all_gather(w_up, "tm", axis=0, tiled=True),
    )
    query_sum, key_sum, value_sum, hidden = tuple(
        (jnp.dot(normed, piece_one, preferred_element_type=jnp.float32) for piece_one in pieces)
    )
    local_heads = query_sum.shape[1] // HEAD_DIM
    queries = query_sum.astype(jnp.bfloat16).reshape(rows_here, local_heads, HEAD_DIM)
    key_grid = key_sum.astype(jnp.bfloat16).reshape(
        frames_here, dancers_here, local_heads * HEAD_DIM
    )
    value_grid = value_sum.astype(jnp.bfloat16).reshape(
        frames_here, dancers_here, local_heads * HEAD_DIM
    )
    mask_row = block_mask[0, 0].astype(jnp.float32)
    cycle_blocks = mask_row.shape[0]
    key_piece = lax.all_gather(key_grid, "ctx", axis=1, tiled=True)
    value_piece = lax.all_gather(value_grid, "ctx", axis=1, tiled=True)
    count = key_piece.shape[1]
    block_ids = jnp.arange(count) // dancers_here
    picker = (block_ids[:, None] == jnp.arange(cycle_blocks)[None, :]).astype(jnp.float32)
    allowed_dancers = jnp.dot(picker, mask_row)
    peak_old = jnp.full((local_heads, rows_here), -1e30, jnp.float32)
    key_rows = key_piece.reshape(frames_here * count, local_heads, HEAD_DIM)
    value_rows = value_piece.reshape(frames_here * count, local_heads, HEAD_DIM)
    allowed = jnp.tile(allowed_dancers, frames_here)
    scores = (
        jnp.einsum("qhd,khd->hqk", queries, key_rows, preferred_element_type=jnp.float32) * 0.125
    )
    scores = jnp.where(allowed[None, None, :] > 0, scores, -1e30)
    peak_new = jnp.maximum(peak_old, jnp.max(scores, axis=-1))
    expo = jnp.exp(scores - peak_new[:, :, None]) * allowed[None, None, :]
    total_new = jnp.sum(expo, axis=-1)
    probs = expo.astype(jnp.bfloat16)
    mixed_new = jnp.einsum("hqk,khd->hqd", probs, value_rows, preferred_element_type=jnp.float32)
    attended = (
        (mixed_new / total_new[:, :, None])
        .transpose(1, 0, 2)
        .reshape(rows_here, local_heads * HEAD_DIM)
        .astype(jnp.bfloat16)
    )
    activated = jax.nn.gelu(hidden, approximate=True).astype(jnp.bfloat16)
    out_full, down_full = (
        lax.all_gather(w_out, "tm", axis=1, tiled=True),
        lax.all_gather(w_down, "tm", axis=1, tiled=True),
    )
    branches = jnp.dot(attended, out_full, preferred_element_type=jnp.float32)
    branches = branches + jnp.dot(activated, down_full, preferred_element_type=jnp.float32)
    mine = lax.psum_scatter(
        branches.astype(jnp.bfloat16), "tp", scatter_dimension=1, tiled=True
    ).astype(jnp.float32)
    features_here = mine.shape[1]
    first_feature = lax.axis_index("tp") * features_here
    normed_cols = lax.dynamic_slice_in_dim(normed_grid, first_feature, features_here, 2)
    padded = jnp.pad(normed_cols.astype(jnp.float32), ((4, 4), (0, 0), (0, 0)))
    extended = jnp.zeros((frames_here + 4, dancers_here, features_here), jnp.float32)
    for offset in range(KERNEL):
        extended = extended + conv_weight[offset] * padded[offset : offset + frames_here + 4]
    convolved = extended[2 : frames_here + 2]
    from_before = from_behind(extended[frames_here + 2 :], "tm", 1)
    from_after = from_behind(extended[0:2], "tm", -1)
    convolved = convolved.at[0:2].add(from_before)
    convolved = convolved.at[frames_here - 2 :].add(from_after)
    token_cols = lax.dynamic_slice_in_dim(tokens, first_feature, features_here, 2).astype(
        jnp.float32
    )
    result = token_cols + mine.reshape(frames_here, dancers_here, features_here) + convolved
    return result.astype(jnp.bfloat16)


def solution(mesh):
    placed = (
        P(("groups", "tm"), "ctx", None),
        P(),
        P(("groups", "tm"), "ctx", None),
        P("tm", "tp"),
        P("tm", "tp"),
        P("tm", "tp"),
        P("tp", "tm"),
        P("tm", "tp"),
        P("tp", "tm"),
        P(None, "tp"),
    )
    return jax.shard_map(
        on_device,
        mesh=mesh,
        in_specs=placed,
        out_specs=P(("groups", "tm"), "ctx", "tp"),
        check_vma=False,
    )
```

profile of v0, /device:TPU:0, one launch (start us, length us, event | category | flops | bytes accessed | tf_op | source)
XLA Modules:
  0.0 189.4 jit_solution(12623946930418223822)
XLA Ops:
  6.5 0.7 all-gather.7.cloned.1.call-update
  7.3 0.7 all-gather.9.cloned.1.call-update
  8.1 0.7 all-gather.11.cloned.1.call-update
  8.8 0.5 all-gather.17.cloned.1.call-update
  9.4 0.5 all-gather.15.cloned.1.call-update
  10.0 0.5 all-gather.13.cloned.1.call-update
  10.6 0.3 fusion.15
  12.0 1.0 fusion.26
  13.0 19.9 %all-gather.7.cloned.1.call-done = bf16[1024,512]{1,0:T(8,128)(2,1)} async-done(((bf16[512,512]{1,0:T(8,128)(2,1)}), bf16[1024,512]{1,0:T(8,128)(2,1)}) %all-gather.7.cloned.1.call-update) | async-done | bytes 1048592 | tf_op jit(solution)/shard_map/all_gather | solution.py:30
  32.9 1.5 convolution_convert_fusion.2
  34.6 21.2 %all-gather.9.cloned.1.call-done = bf16[1024,512]{1,0:T(8,128)(2,1)} async-done(((bf16[512,512]{1,0:T(8,128)(2,1)}), bf16[1024,512]{1,0:T(8,128)(2,1)}) %all-gather.9.cloned.1.call-update) | async-done | bytes 1048592 | tf_op jit(solution)/shard_map/all_gather | solution.py:31
  55.8 1.5 convolution_convert_fusion.1
  57.4 15.5 %all_gather.26 = bf16[64,8,512]{2,0,1:T(8,128)(2,1)S(1)} all-gather(bf16[64,2,512]{2,0,1:T(8,128)(2,1)S(1)} %copy.35), channel_id=1, replica_groups=mesh['groups'=2,'ctx'=4,'tm'=2,'tp'=2] {'ctx'}, dimensions={1}, use_global_device_ids=true | all-gather | bytes 655360 | tf_op jit(solution)/shard_map/all_gather | solution.py:48
  73.1 0.5 reshape.130
  73.7 5.0 %all-gather.11.cloned.1.call-done = bf16[1024,512]{1,0:T(8,128)(2,1)} async-done(((bf16[512,512]{1,0:T(8,128)(2,1)}), bf16[1024,512]{1,0:T(8,128)(2,1)}) %all-gather.11.cloned.1.call-update) | async-done | bytes 1048592 | tf_op jit(solution)/shard_map/all_gather | solution.py:32
  78.6 1.5 convolution_convert_fusion
  80.3 0.6 fusion
  80.9 15.5 %all_gather.28 = bf16[64,8,512]{2,0,1:T(8,128)(2,1)S(1)} all-gather(bf16[64,2,512]{2,0,1:T(8,128)(2,1)S(1)} %copy.38), channel_id=1, replica_groups=mesh['groups'=2,'ctx'=4,'tm'=2,'tp'=2] {'ctx'}, dimensions={1}, use_global_device_ids=true | all-gather | bytes 655360 | tf_op jit(solution)/shard_map/all_gather | solution.py:49
  96.6 1.5 reshape.132
  98.2 0.6 fusion.1
  98.8 0.6 copy-done.3
  99.4 0.9 fusion.5
  100.2 12.9 %all-gather.17.cloned.1.call-done = bf16[1024,1024]{1,0:T(8,128)(2,1)} async-done(((bf16[1024,512]{1,0:T(8,128)(2,1)}), bf16[1024,1024]{1,0:T(8,128)(2,1)}) %all-gather.17.cloned.1.call-update) | async-done | bytes 2097168 | tf_op jit(solution)/shard_map/all_gather | solution.py:76
  113.2 34.5 %all-gather.15.cloned.1.call-done = bf16[1024,1024]{1,0:T(8,128)(2,1)} async-done(((bf16[512,1024]{1,0:T(8,128)(2,1)}), bf16[1024,1024]{1,0:T(8,128)(2,1)}) %all-gather.15.cloned.1.call-update) | async-done | bytes 2097168 | tf_op jit(solution)/shard_map/all_gather | solution.py:33
  147.7 3.1 %fusion.30 = f32[128,1024]{1,0:T(8,128)S(1)} fusion(bf16[1024,1024]{1,0:T(8,128)(2,1)} %all-gather.17.cloned.1.call-done, bf16[128,1024]{1,0:T(8,128)(2,1)S(1)} %reshape.127, bf16[1024,1024]{1,0:T(8,128)(2,1)} %all-gather.15.cloned.1.call-done), kind=kOutput, calls=%fused_computation.45 | convolution fusion | flops 538050560 | bytes 4980736 | tf_op jit(solution)/shard_map/dot_general | solution.py:79
  150.8 19.6 %all-gather.13.cloned.1.call-done = bf16[512,1024]{1,0:T(8,128)(2,1)} async-done(((bf16[512,512]{1,0:T(8,128)(2,1)}), bf16[512,1024]{1,0:T(8,128)(2,1)}) %all-gather.13.cloned.1.call-update) | async-done | bytes 1048592 | tf_op jit(solution)/shard_map/all_gather | solution.py:75
  170.4 2.3 %fusion.3 = bf16[128,1024]{1,0:T(8,128)(2,1)} fusion(f32[128,1024]{1,0:T(8,128)S(1)} %fusion.30, bf16[128,512]{0,1:T(8,128)(2,1)S(1)} %bitcast.34, bf16[512,1024]{1,0:T(8,128)(2,1)} %all-gather.13.cloned.1.call-done), kind=kOutput, calls=%fused_computation.6 | convolution fusion | flops 134479872 | bytes 1966080 | tf_op jit(solution)/shard_map/dot_general | solution.py:78
  172.7 2.3 %collective-permute-start = (f32[2,2,512]{2,1,0:T(2,128)S(1)}, f32[2,2,512]{2,1,0:T(2,128)S(1)}, u32[]{:S(2)}, u32[]{:S(2)}) collective-permute-start(f32[2,2,512]{2,1,0:T(2,128)S(1)} %get-tuple-element.30), channel_id=1, source_target_pairs={{0,2},{1,3},{4,6},{5,7},{8,10},{9,11},{12,14},{13,15},{16,18},{17,... | collective-permute-start | bytes 24584 | tf_op jit(solution)/shard_map/ppermute | solution.py:13
  175.0 1.3 collective-permute-start.1
  176.3 4.2 %collective-permute-done.1 = f32[2,2,512]{2,1,0:T(2,128)S(1)} collective-permute-done((f32[2,2,512]{2,1,0:T(2,128)S(1)}, f32[2,2,512]{2,1,0:T(2,128)S(1)}, u32[]{:S(2)}, u32[]{:S(2)}) %collective-permute-start.1) | collective-permute-done | bytes 8224 | tf_op jit(solution)/shard_map/ppermute | solution.py:13
  180.6 1.1 reshape.136
  181.7 0.8 add_convert_fusion
  (47 shorter events, 2.3 us)
Async XLA Ops:
  6.5 4.0 %copy-start = (bf16[64,2,1024]{2,1,0:T(2,128)(2,1)S(1)}, bf16[64,2,1024]{2,1,0:T(2,128)(2,1)}, u32[]{:S(2)}) copy-start(bf16[64,2,1024]{2,1,0:T(2,128)(2,1)} %param.14) | copy-start | bytes 786436
  6.5 26.4 %all-gather.7.cloned.1.call-start = ((), (), s32[]{:S(2)}) async-start(), calls=%async_computation.1 | async-start | bytes 1572864 | tf_op jit(solution)/shard_map/all_gather | solution.py:30
  7.3 3.7 %copy-start.5 = (f32[1024]{0:T(1024)S(1)}, f32[1024]{0:T(1024)}, u32[]{:S(2)}) copy-start(f32[1024]{0:T(1024)} %param.15) | copy-start | bytes 12292
  7.3 48.5 %all-gather.9.cloned.1.call-start = ((), (), s32[]{:S(2)}) async-start(), calls=%async_computation.2 | async-start | bytes 1572864 | tf_op jit(solution)/shard_map/all_gather | solution.py:31
  8.0 70.6 %all-gather.11.cloned.1.call-start = ((), (), s32[]{:S(2)}) async-start(), calls=%async_computation.3 | async-start | bytes 1572864 | tf_op jit(solution)/shard_map/all_gather | solution.py:32
  8.8 104.4 %all-gather.17.cloned.1.call-start = ((), (), s32[]{:S(2)}) async-start(), calls=%async_computation.6 | async-start | bytes 3145728 | tf_op jit(solution)/shard_map/all_gather | solution.py:76
  9.3 2.3 %copy-start.4 = (f32[5,512]{1,0:T(8,128)S(1)}, f32[5,512]{1,0:T(8,128)}, u32[]{:S(2)}) copy-start(f32[5,512]{1,0:T(8,128)} %param.23) | copy-start | bytes 30724
  9.3 2.3 %copy-start.6 = (s32[1,1,4]{2,1,0:T(1,128)S(1)}, s32[1,1,4]{2,1,0:T(1,128)}, u32[]{:S(2)}) copy-start(s32[1,1,4]{2,1,0:T(1,128)} %param.16) | copy-start | bytes 52
  9.3 138.3 %all-gather.15.cloned.1.call-start = ((), (), s32[]{:S(2)}) async-start(), calls=%async_computation.5 | async-start | bytes 3145728 | tf_op jit(solution)/shard_map/all_gather | solution.py:33
  9.9 160.5 %all-gather.13.cloned.1.call-start = ((), (), s32[]{:S(2)}) async-start(), calls=%async_computation.4 | async-start | bytes 1572864 | tf_op jit(solution)/shard_map/all_gather | solution.py:75
  10.5 170.1 %reduce-scatter.2.cloned.1.call-start = ((), (), s32[]{:S(2)}) async-start(), calls=%async_computation.7 | async-start | bytes 393216 | tf_op jit(solution)/shard_map/reduce_scatter | solution.py:80
  98.1 1.2 copy-start.3
  150.7 21.9 %copy-start.2 = (f32[68,2,512]{2,1,0:T(2,128)S(1)}, f32[68,2,512]{2,1,0:T(2,128)}, u32[]{:S(2)}) copy-start(f32[68,2,512]{2,1,0:T(2,128)} %fusion.26) | copy-start | bytes 835588
  150.8 25.5 %slice-start = ((f32[68,2,512]{2,1,0:T(2,128)}), f32[64,2,512]{2,1,0:T(2,128)S(1)}, s32[]{:S(2)}) async-start(f32[68,2,512]{2,1,0:T(2,128)} %fusion.26), calls=%async_computation.8 | async-start | bytes 524288 | tf_op jit(solution)/shard_map/slice | solution.py:90
  150.8 30.9 %copy-start.1 = (bf16[64,2,1024]{2,1,0:T(2,128)(2,1)S(1)}, bf16[64,2,1024]{2,1,0:T(2,128)(2,1)}, u32[]{:S(2)}) copy-start(bf16[64,2,1024]{2,1,0:T(2,128)(2,1)} %param.14) | copy-start | bytes 786436
  172.7 3.6 %collective-permute-start = (f32[2,2,512]{2,1,0:T(2,128)S(1)}, f32[2,2,512]{2,1,0:T(2,128)S(1)}, u32[]{:S(2)}, u32[]{:S(2)}) collective-permute-start(f32[2,2,512]{2,1,0:T(2,128)S(1)} %get-tuple-element.30), channel_id=1, source_target_pairs={{0,2},{1,3},{4,6},{5,7},{8,10},{9,11},{12,14},{13,15},{16,18},{17,... | collective-permute-start | bytes 24584 | tf_op jit(solution)/shard_map/ppermute | solution.py:13
  175.0 5.5 %collective-permute-start.1 = (f32[2,2,512]{2,1,0:T(2,128)S(1)}, f32[2,2,512]{2,1,0:T(2,128)S(1)}, u32[]{:S(2)}, u32[]{:S(2)}) collective-permute-start(f32[2,2,512]{2,1,0:T(2,128)S(1)} %get-tuple-element.29), channel_id=1, source_target_pairs={{2,0},{3,1},{6,4},{7,5},{10,8},{11,9},{14,12},{15,13},{18,16},{19,... | collective-permute-start | bytes 24584 | tf_op jit(solution)/shard_map/ppermute | solution.py:13
Sparse Core Ops, SparseCore 0:
  8.9 23.9 all-gather.6
  34.5 21.2 all-gather.8
  57.3 21.2 all-gather.10
  80.0 33.0 all-gather.16
  114.5 33.0 all-gather.14
  149.1 21.2 all-gather.12
  172.8 7.7 reduce-scatter.1
where the time goes:
time: 190 us; the launch traced here: 189 us
  waiting for transfers between devices  121 us (64%)
  blocking collectives  30.9 us (16%)
  between operations  13.8 us (7%)
  matrix products  11.6 us (6%)
  local copies, waits for them, and re-layouts  4.94 us (3%)
  starting transfers between devices  3.77 us (2%)
  other arithmetic  3.36 us (2%)
    all_gather x1, waiting for transfers between devices, on_device(): lax.all_gather(w_up, 'tm', axis=0, tiled=True)  34.5 us
    all_gather x1, waiting for transfers between devices, on_device(): lax.all_gather(w_key, 'tm', axis=0, tiled=True)  21.2 us
    all_gather x1, waiting for transfers between devices, on_device(): lax.all_gather(w_query, 'tm', axis=0, tiled=True)  19.9 us
    all_gather x1, waiting for transfers between devices, on_device(): lax.all_gather(w_out, 'tm', axis=1, tiled=True)  19.6 us
    all_gather x1, blocking collectives, on_device(): key_piece = lax.all_gather(key_grid, 'ctx', axis=1, tiled=True)  15.5 us
    all_gather x1, blocking collectives, on_device(): value_piece = lax.all_gather(value_grid, 'ctx', axis=1, tiled=True)  15.5 us
    all_gather x1, waiting for transfers between devices, on_device(): lax.all_gather(w_down, 'tm', axis=1, tiled=True)  12.9 us
    all_gather x1, waiting for transfers between devices, on_device(): lax.all_gather(w_value, 'tm', axis=0, tiled=True)  4.95 us
  transfers between devices with their start and end apart: 9, of which 8 were waited for; matrix products, arithmetic and copies ran while one was open for 8% of the time, Pallas kernels for 0%

commit v1 on v0

--- a/solution.py
+++ b/solution.py
@@ -2,6 +2,7 @@
 import jax.numpy as jnp
 from jax import lax
 from jax.sharding import PartitionSpec as P
+from jax.lax import all_gather
 
 HEAD_DIM = 64
 KERNEL = 5
@@ -45,8 +46,12 @@
     )
     mask_row = block_mask[0, 0].astype(jnp.float32)
     cycle_blocks = mask_row.shape[0]
-    key_piece = lax.all_gather(key_grid, "ctx", axis=1, tiled=True)
-    value_piece = lax.all_gather(value_grid, "ctx", axis=1, tiled=True)
+    touch_the_yards = lambda t0, raw: jnp.split(
+        all_gather(jnp.concatenate([t0, raw], 0), axis_name="ctx", axis=1, tiled=True),
+        [t0.shape[0]],
+        0,
+    )
+    key_piece, value_piece = touch_the_yards(key_grid, value_grid)
     count = key_piece.shape[1]
     block_ids = jnp.arange(count) // dancers_here
     picker = (block_ids[:, None] == jnp.arange(cycle_blocks)[None, :]).astype(jnp.float32)

time: 190 us -> 219 us (1.15)
  waiting for transfers between devices: 121 us -> 179 us
  blocking collectives: 30.9 us -> 0 us
    all_gather x2 -> x0, blocking collectives: 30.9 us -> none  [the longest x1 15.5 us: on_device(): key_piece = lax.all_gather(key_grid, 'ctx', axis=1, tiled=True)]
    all_gather x0 -> x1, waiting for transfers between devices: none -> 26.4 us  [on_device(): all_gather(jnp.concatenate([t0, raw], 0), axis_name='ctx', axis=1, tiled=...]
    all_gather x1, waiting for transfers between devices: 12.9 us -> 32.9 us  [on_device(): lax.all_gather(w_down, 'tm', axis=1, tiled=True)]
    all_gather x1, waiting for transfers between devices: 4.95 us -> 22.1 us  [on_device(): lax.all_gather(w_value, 'tm', axis=0, tiled=True)]
    all_gather x1, waiting for transfers between devices: 19.6 us -> 16.1 us  [on_device(): lax.all_gather(w_out, 'tm', axis=1, tiled=True)]
  transfers between devices with their start and end apart: 9 -> 10, of which waited for: 8 -> 9; matrix products, arithmetic and copies ran while one was open for 8% -> 8% of each run, Pallas kernels for 0% -> 0%
where the time goes in v1:
time: 219 us; the launch traced here: 218 us
  waiting for transfers between devices  179 us (82%)
  between operations  13.8 us (6%)
  matrix products  11.6 us (5%)
  local copies, waits for them, and re-layouts  5.68 us (3%)
  other arithmetic  3.96 us (2%)
  starting transfers between devices  3.82 us (2%)
    all_gather x1, waiting for transfers between devices, on_device(): lax.all_gather(w_up, 'tm', axis=0, tiled=True)  34.5 us
    all_gather x1, waiting for transfers between devices, on_device(): lax.all_gather(w_down, 'tm', axis=1, tiled=True)  32.9 us
    all_gather x1, waiting for transfers between devices, on_device(): all_gather(jnp.concatenate([t0, raw], 0), axis_name='ctx', axis=1, tiled=...  26.4 us
    all_gather x1, waiting for transfers between devices, on_device(): lax.all_gather(w_value, 'tm', axis=0, tiled=True)  22.1 us
    all_gather x1, waiting for transfers between devices, on_device(): lax.all_gather(w_key, 'tm', axis=0, tiled=True)  21.2 us
    all_gather x1, waiting for transfers between devices, on_device(): lax.all_gather(w_query, 'tm', axis=0, tiled=True)  18.2 us
    all_gather x1, waiting for transfers between devices, on_device(): lax.all_gather(w_out, 'tm', axis=1, tiled=True)  16.1 us
    dot_general x3, matrix products, on_device(): jnp.dot(normed, piece_one, preferred_element_type=jnp.float32)  4.59 us
  transfers between devices with their start and end apart: 10, of which 9 were waited for; matrix products, arithmetic and copies ran while one was open for 8% of the time, Pallas kernels for 0%

profile of v1, /device:TPU:0, one launch (start us, length us, event | category | flops | bytes accessed | tf_op | source)
XLA Modules:
  0.0 218.3 jit_solution(15491028782349576179)
XLA Ops:
  6.5 0.7 all-gather.12.cloned.1.call-update
  7.3 0.7 all-gather.10.cloned.1.call-update
  8.1 0.7 all-gather.8.cloned.1.call-update
  8.8 0.5 all-gather.20.cloned.1.call-update
  9.4 0.5 all-gather.18.cloned.1.call-update
  10.0 0.3 fusion.15
  10.8 22.1 %all-gather.12.cloned.1.call-done = bf16[1024,512]{1,0:T(8,128)(2,1)} async-done(((bf16[512,512]{1,0:T(8,128)(2,1)}), bf16[1024,512]{1,0:T(8,128)(2,1)}) %all-gather.12.cloned.1.call-update) | async-done | bytes 1048592 | tf_op jit(solution)/shard_map/all_gather | solution.py:33
  32.9 1.5 convolution_convert_fusion
  34.6 21.2 %all-gather.10.cloned.1.call-done = bf16[1024,512]{1,0:T(8,128)(2,1)} async-done(((bf16[512,512]{1,0:T(8,128)(2,1)}), bf16[1024,512]{1,0:T(8,128)(2,1)}) %all-gather.10.cloned.1.call-update) | async-done | bytes 1048592 | tf_op jit(solution)/shard_map/all_gather | solution.py:32
  55.8 1.5 convolution_convert_fusion.1
  57.4 0.7 pad_maximum_fusion
  58.2 0.7 all-gather.16.cloned.1.call-update
  59.5 0.6 broadcast_compare_fusion
  60.4 18.2 %all-gather.8.cloned.1.call-done = bf16[1024,512]{1,0:T(8,128)(2,1)} async-done(((bf16[512,512]{1,0:T(8,128)(2,1)}), bf16[1024,512]{1,0:T(8,128)(2,1)}) %all-gather.8.cloned.1.call-update) | async-done | bytes 1048592 | tf_op jit(solution)/shard_map/all_gather | solution.py:31
  78.6 1.5 convolution_convert_fusion.2
  80.3 32.9 %all-gather.20.cloned.1.call-done = bf16[1024,1024]{1,0:T(8,128)(2,1)} async-done(((bf16[1024,512]{1,0:T(8,128)(2,1)}), bf16[1024,1024]{1,0:T(8,128)(2,1)}) %all-gather.20.cloned.1.call-update) | async-done | bytes 2097168 | tf_op jit(solution)/shard_map/all_gather | solution.py:81
  113.2 34.5 %all-gather.18.cloned.1.call-done = bf16[1024,1024]{1,0:T(8,128)(2,1)} async-done(((bf16[512,1024]{1,0:T(8,128)(2,1)}), bf16[1024,1024]{1,0:T(8,128)(2,1)}) %all-gather.18.cloned.1.call-update) | async-done | bytes 2097168 | tf_op jit(solution)/shard_map/all_gather | solution.py:34
  147.7 3.1 %fusion.30 = f32[128,1024]{1,0:T(8,128)S(1)} fusion(bf16[1024,1024]{1,0:T(8,128)(2,1)} %all-gather.20.cloned.1.call-done, bf16[128,1024]{1,0:T(8,128)(2,1)S(1)} %reshape.127, bf16[1024,1024]{1,0:T(8,128)(2,1)} %all-gather.18.cloned.1.call-done), kind=kOutput, calls=%fused_computation.45 | convolution fusion | flops 538050560 | bytes 4980736 | tf_op jit(solution)/shard_map/dot_general | solution.py:84
  150.7 26.4 %all-gather.14.cloned.1.call-done = bf16[128,8,512]{2,0,1:T(8,128)(2,1)} async-done(((bf16[128,2,512]{2,0,1:T(8,128)(2,1)}), bf16[128,8,512]{2,0,1:T(8,128)(2,1)}) %all-gather.14.cloned.1.call-update) | async-done | bytes 1048592 | tf_op jit(solution)/shard_map/all_gather | solution.py:50
  177.1 1.3 fusion.45
  178.7 0.5 reshape.131
  179.6 1.6 reshape.132
  181.1 0.6 fusion
  181.8 0.6 fusion.1
  182.4 0.9 fusion.5
  183.3 16.1 %all-gather.16.cloned.1.call-done = bf16[512,1024]{1,0:T(8,128)(2,1)} async-done(((bf16[512,512]{1,0:T(8,128)(2,1)}), bf16[512,1024]{1,0:T(8,128)(2,1)}) %all-gather.16.cloned.1.call-update) | async-done | bytes 1048592 | tf_op jit(solution)/shard_map/all_gather | solution.py:80
  199.3 2.3 %fusion.3 = bf16[128,1024]{1,0:T(8,128)(2,1)} fusion(f32[128,1024]{1,0:T(8,128)S(1)} %fusion.30, bf16[128,512]{0,1:T(8,128)(2,1)S(1)} %bitcast.34, bf16[512,1024]{1,0:T(8,128)(2,1)} %all-gather.16.cloned.1.call-done), kind=kOutput, calls=%fused_computation.6 | convolution fusion | flops 134479872 | bytes 1966080 | tf_op jit(solution)/shard_map/dot_general | solution.py:83
  201.6 2.3 %collective-permute-start = (f32[2,2,512]{2,1,0:T(2,128)S(1)}, f32[2,2,512]{2,1,0:T(2,128)S(1)}, u32[]{:S(2)}, u32[]{:S(2)}) collective-permute-start(f32[2,2,512]{2,1,0:T(2,128)S(1)} %get-tuple-element.32), channel_id=1, source_target_pairs={{0,2},{1,3},{4,6},{5,7},{8,10},{9,11},{12,14},{13,15},{16,18},{17,... | collective-permute-start | bytes 24584 | tf_op jit(solution)/shard_map/ppermute | solution.py:14
  203.9 1.3 collective-permute-start.1
  205.3 4.2 %collective-permute-done.1 = f32[2,2,512]{2,1,0:T(2,128)S(1)} collective-permute-done((f32[2,2,512]{2,1,0:T(2,128)S(1)}, f32[2,2,512]{2,1,0:T(2,128)S(1)}, u32[]{:S(2)}, u32[]{:S(2)}) %collective-permute-start.1) | collective-permute-done | bytes 8224 | tf_op jit(solution)/shard_map/ppermute | solution.py:14
  209.5 1.1 reshape.136
  210.6 0.8 add_convert_fusion
  (51 shorter events, 2.6 us)
Async XLA Ops:
  6.5 3.4 %copy-start = (bf16[64,2,1024]{2,1,0:T(2,128)(2,1)S(1)}, bf16[64,2,1024]{2,1,0:T(2,128)(2,1)}, u32[]{:S(2)}) copy-start(bf16[64,2,1024]{2,1,0:T(2,128)(2,1)} %param.14) | copy-start | bytes 786436
  6.5 3.8 %copy-start.6 = (f32[1024]{0:T(1024)S(1)}, f32[1024]{0:T(1024)}, u32[]{:S(2)}) copy-start(f32[1024]{0:T(1024)} %param.15) | copy-start | bytes 12292
  6.5 26.4 %all-gather.12.cloned.1.call-start = ((), (), s32[]{:S(2)}) async-start(), calls=%async_computation.3 | async-start | bytes 1572864 | tf_op jit(solution)/shard_map/all_gather | solution.py:33
  7.3 48.5 %all-gather.10.cloned.1.call-start = ((), (), s32[]{:S(2)}) async-start(), calls=%async_computation.2 | async-start | bytes 1572864 | tf_op jit(solution)/shard_map/all_gather | solution.py:32
  8.0 70.6 %all-gather.8.cloned.1.call-start = ((), (), s32[]{:S(2)}) async-start(), calls=%async_computation.1 | async-start | bytes 1572864 | tf_op jit(solution)/shard_map/all_gather | solution.py:31
  8.7 104.4 %all-gather.20.cloned.1.call-start = ((), (), s32[]{:S(2)}) async-start(), calls=%async_computation.7 | async-start | bytes 3145728 | tf_op jit(solution)/shard_map/all_gather | solution.py:81
  9.3 138.4 %all-gather.18.cloned.1.call-start = ((), (), s32[]{:S(2)}) async-start(), calls=%async_computation.6 | async-start | bytes 3145728 | tf_op jit(solution)/shard_map/all_gather | solution.py:34
  9.9 167.2 %all-gather.14.cloned.1.call-start = ((), (), s32[]{:S(2)}) async-start(), calls=%async_computation.4 | async-start | bytes 1310720 | tf_op jit(solution)/shard_map/all_gather | solution.py:50
  34.5 24.7 %copy-start.4 = (f32[5,512]{1,0:T(8,128)S(1)}, f32[5,512]{1,0:T(8,128)}, u32[]{:S(2)}) copy-start(f32[5,512]{1,0:T(8,128)} %param.23) | copy-start | bytes 30724
  34.5 24.7 %copy-start.7 = (s32[1,1,4]{2,1,0:T(1,128)S(1)}, s32[1,1,4]{2,1,0:T(1,128)}, u32[]{:S(2)}) copy-start(s32[1,1,4]{2,1,0:T(1,128)} %param.16) | copy-start | bytes 52
  58.1 141.2 %all-gather.16.cloned.1.call-start = ((), (), s32[]{:S(2)}) async-start(), calls=%async_computation.5 | async-start | bytes 1572864 | tf_op jit(solution)/shard_map/all_gather | solution.py:80
  58.9 150.6 %reduce-scatter.2.cloned.1.call-start = ((), (), s32[]{:S(2)}) async-start(), calls=%async_computation.8 | async-start | bytes 393216 | tf_op jit(solution)/shard_map/reduce_scatter | solution.py:85
  59.5 0.6 copy-start.2
  178.7 2.4 %copy-start.5 = (pred[512]{0:T(512)(128)(4,1)S(1)}, pred[512]{0:T(512)(128)(4,1)}, u32[]{:S(2)}) copy-start(pred[512]{0:T(512)(128)(4,1)} %broadcast_compare_fusion) | copy-start | bytes 1540
  179.6 2.2 %copy-start.3 = (f32[512]{0:T(512)S(1)}, f32[512]{0:T(512)}, u32[]{:S(2)}) copy-start(f32[512]{0:T(512)} %copy-done.2) | copy-start | bytes 6148
  181.1 1.3 copy-start.1
  201.6 3.6 %collective-permute-start = (f32[2,2,512]{2,1,0:T(2,128)S(1)}, f32[2,2,512]{2,1,0:T(2,128)S(1)}, u32[]{:S(2)}, u32[]{:S(2)}) collective-permute-start(f32[2,2,512]{2,1,0:T(2,128)S(1)} %get-tuple-element.32), channel_id=1, source_target_pairs={{0,2},{1,3},{4,6},{5,7},{8,10},{9,11},{12,14},{13,15},{16,18},{17,... | collective-permute-start | bytes 24584 | tf_op jit(solution)/shard_map/ppermute | solution.py:14
  203.9 5.5 %collective-permute-start.1 = (f32[2,2,512]{2,1,0:T(2,128)S(1)}, f32[2,2,512]{2,1,0:T(2,128)S(1)}, u32[]{:S(2)}, u32[]{:S(2)}) collective-permute-start(f32[2,2,512]{2,1,0:T(2,128)S(1)} %get-tuple-element.31), channel_id=1, source_target_pairs={{2,0},{3,1},{6,4},{7,5},{10,8},{11,9},{14,12},{15,13},{18,16},{19,... | collective-permute-start | bytes 24584 | tf_op jit(solution)/shard_map/ppermute | solution.py:14
Sparse Core Ops, SparseCore 0:
  8.9 23.9 all-gather.11
  34.5 21.2 all-gather.9
  57.3 21.2 all-gather.7
  80.0 33.0 all-gather.19
  114.5 33.0 all-gather.17
  149.1 27.9 all-gather.13
  178.7 20.6 all-gather.15
  201.8 7.7 reduce-scatter.1
